TPU v7x, 256 devices: a whole 4x4x8 slice. The times are simulated.
256 devices in a mesh: row: 8 (over y, core), col: 32 (over z, x).
Axes of the slice: x: 4, y: 4, z: 8, core: 2. Of those that a mesh axis runs over, the one named last changes fastest.
Arguments:
- row_points: float32 [64, 16384], P(None, 'row'), may hold values from -6 to 6
- panel_points: float32 [64, 1024], P(None, 'col'), may hold values from -6 to 6
- scales: float32 [64], replicated, may hold values from 0.005 to 0.03
Outputs:
- diag_factor: float32 [1024, 1024], P('row', 'col')
- panel_factor_t: float32 [1024, 16384], P('col', 'row')
- updated_ahead_t: float32 [1024, 16384], P('col', 'row')
All inputs are finite; a program needn't handle non-finite values.
Results may differ from a plain program's by a relative error of at most 0.0003.
Values sent between devices are 32-bit elements; how exact they have to be, the bound alone decides.
No kernel may reach another device: no remote copies, remote signals or barrier semaphores. Data moves between devices by JAX's collectives and lax.ppermute only.
A program may use at most 128 MiB of HBM per device.

v0:
```python
import jax
import jax.numpy as jnp
from jax import lax
from jax.sharding import PartitionSpec as P

B = 1024
RIDGE = 0.5


def spread(block, axis, holder):
    block = jnp.where(lax.axis_index(axis) == holder, block, jnp.zeros_like(block))
    return lax.psum(block, axis)


def kernel_block(sources, targets, scales):
    weighted = sources * scales[:, None]
    source_sq = jnp.sum(weighted * sources, axis=0)
    target_sq = jnp.sum(targets * targets * scales[:, None], axis=0)
    cross = lax.dot_general(
        weighted,
        targets,
        (((0,), (0,)), ((), ())),
        precision=lax.Precision.HIGHEST,
        preferred_element_type=jnp.float32,
    )
    return jnp.exp(2.0 * cross - source_sq[:, None] - target_sq[None, :])


def times_left(matrix, pieces):
    return jnp.dot(
        matrix, pieces, precision=lax.Precision.HIGHEST, preferred_element_type=jnp.float32
    )


def transposed_times(matrix, pieces):
    return lax.dot_general(
        matrix,
        pieces,
        (((0,), (0,)), ((), ())),
        precision=lax.Precision.HIGHEST,
        preferred_element_type=jnp.float32,
    )


def body(row_points, panel_points, scales):
    n_col = lax.axis_size("col")
    n_row = lax.axis_size("row")
    col_index = lax.axis_index("col")
    row_index = lax.axis_index("row")
    col_share = B // n_col
    row_share = B // n_row
    rows_dev = row_points.shape[1]
    all_panel = lax.all_gather(panel_points, "col", axis=1, tiled=True)
    first_col = col_index * col_share
    root_row = first_col // rows_dev
    local_look = lax.dynamic_slice_in_dim(row_points, first_col % rows_dev, col_share, 1)
    look_points = spread(local_look, "row", root_row)
    identity = jnp.eye(B, dtype=jnp.float32)
    diag_block = kernel_block(all_panel, all_panel, scales) + RIDGE * identity
    diag_full = jnp.linalg.cholesky(diag_block)
    inverse = lax.linalg.triangular_solve(diag_full, identity, left_side=True, lower=True)
    own_inverse = lax.dynamic_slice_in_dim(inverse, first_col, col_share, 0)
    look_kernel = kernel_block(all_panel, look_points, scales)
    look_factor = times_left(inverse, look_kernel)
    look_rows = kernel_block(look_points, row_points, scales)
    own_kernel = kernel_block(panel_points, row_points, scales)
    panel_tile = times_left(own_inverse, lax.all_gather(own_kernel, "col", axis=0, tiled=True))
    reduction = transposed_times(look_factor, lax.all_gather(panel_tile, "col", axis=0, tiled=True))
    updated = look_rows - reduction
    diag_tile = lax.dynamic_slice(
        diag_full, (row_index * row_share, first_col), (row_share, col_share)
    )
    return (diag_tile, panel_tile, updated)


def solution(mesh):
    return jax.shard_map(
        body,
        mesh=mesh,
        in_specs=(P(None, "row"), P(None, "col"), P()),
        out_specs=(P("row", "col"), P("col", "row"), P("col", "row")),
        check_vma=False,
    )
```

profile of v0, /device:TPU:1, one launch (start us, length us, event | category | flops | bytes accessed | tf_op | source)
XLA Modules:
  0.0 573.6 jit_solution(7809796819884871075)
XLA Ops:
  8.1 23.8 %psum.7 = f32[64,32]{0,1:T(8,128)S(1)} all-reduce(f32[64,32]{0,1:T(8,128)S(1)} %broadcast_select_fusion), channel_id=1, replica_groups=mesh['row'=8,'col'=32] {'row'}, use_global_device_ids=true, to_apply=%region_20.21 | all-reduce | flops 2048 | bytes 16384 | tf_op jit(solution)/shard_map/psum | solution.py:12
  36.3 42.3 %all_gather.9 = f32[64,1024]{0,1:T(8,128)S(1)} all-gather(f32[64,32]{0,1:T(8,128)} %param.4), channel_id=1, replica_groups=mesh['row'=8,'col'=32] {'col'}, dimensions={1}, use_global_device_ids=true | all-gather | bytes 270336 | tf_op jit(solution)/shard_map/all_gather | solution.py:53
  79.6 4.1 fusion.38
  85.7 2.7 fusion.1
  88.4 5.5 copy.6
  93.8 4.9 add_multiply_fusion
  100.8 11.7 %cholesky.222 = f32[128,128]{1,0:T(8,128)S(1)} custom-call(f32[128,128]{1,0:T(8,128)S(1)} %cholesky.577), custom_call_target="Cholesky" | custom-call | tf_op jit(solution)/shard_map/jit(cholesky)/cholesky | solution.py:60
  112.5 9.8 %custom-call.62 = f32[1,128,128]{1,2,0:T(8,128)S(1)} custom-call(f32[1,128,128]{2,1,0:T(8,128)S(1)} %get-tuple-element.77), custom_call_target="InvertDiagBlocksLowerTriangular" | custom-call | tf_op jit(solution)/shard_map/jit(cholesky)/cholesky | solution.py:60
  124.2 2.5 cholesky.254
  128.6 11.7 %cholesky.243 = f32[128,128]{1,0:T(8,128)S(1)} custom-call(f32[128,128]{1,0:T(8,128)S(1)} %cholesky.581), custom_call_target="Cholesky" | custom-call | tf_op jit(solution)/shard_map/jit(cholesky)/cholesky | solution.py:60
  141.8 10.0 %custom-call.63 = f32[1,128,128]{1,2,0:T(8,128)S(1)} custom-call(f32[1,128,128]{2,1,0:T(8,128)S(1)} %get-tuple-element.74), custom_call_target="InvertDiagBlocksLowerTriangular" | custom-call | tf_op jit(solution)/shard_map/jit(cholesky)/cholesky | solution.py:60
  155.1 11.7 %cholesky.466 = f32[128,128]{1,0:T(8,128)S(1)} custom-call(f32[128,128]{1,0:T(8,128)S(1)} %cholesky.586), custom_call_target="Cholesky" | custom-call | tf_op jit(solution)/shard_map/jit(cholesky)/cholesky | solution.py:60
  167.5 9.8 %custom-call.64 = f32[1,128,128]{1,2,0:T(8,128)S(1)} custom-call(f32[1,128,128]{2,1,0:T(8,128)S(1)} %get-tuple-element.71), custom_call_target="InvertDiagBlocksLowerTriangular" | custom-call | tf_op jit(solution)/shard_map/jit(cholesky)/cholesky | solution.py:60
  180.9 12.1 %cholesky.485 = f32[128,128]{1,0:T(8,128)S(1)} custom-call(f32[128,128]{1,0:T(8,128)S(1)} %cholesky.591), custom_call_target="Cholesky" | custom-call | tf_op jit(solution)/shard_map/jit(cholesky)/cholesky | solution.py:60
  193.6 9.8 %custom-call.65 = f32[1,128,128]{1,2,0:T(8,128)S(1)} custom-call(f32[1,128,128]{2,1,0:T(8,128)S(1)} %get-tuple-element.68), custom_call_target="InvertDiagBlocksLowerTriangular" | custom-call | tf_op jit(solution)/shard_map/jit(cholesky)/cholesky | solution.py:60
  206.9 11.7 %cholesky.504 = f32[128,128]{1,0:T(8,128)S(1)} custom-call(f32[128,128]{1,0:T(8,128)S(1)} %cholesky.596), custom_call_target="Cholesky" | custom-call | tf_op jit(solution)/shard_map/jit(cholesky)/cholesky | solution.py:60
  219.2 9.8 %custom-call.66 = f32[1,128,128]{1,2,0:T(8,128)S(1)} custom-call(f32[1,128,128]{2,1,0:T(8,128)S(1)} %get-tuple-element.65), custom_call_target="InvertDiagBlocksLowerTriangular" | custom-call | tf_op jit(solution)/shard_map/jit(cholesky)/cholesky | solution.py:60
  232.5 11.7 %cholesky.524 = f32[128,128]{1,0:T(8,128)S(1)} custom-call(f32[128,128]{1,0:T(8,128)S(1)} %cholesky.601), custom_call_target="Cholesky" | custom-call | tf_op jit(solution)/shard_map/jit(cholesky)/cholesky | solution.py:60
  244.9 9.8 %custom-call.67 = f32[1,128,128]{1,2,0:T(8,128)S(1)} custom-call(f32[1,128,128]{2,1,0:T(8,128)S(1)} %get-tuple-element.62), custom_call_target="InvertDiagBlocksLowerTriangular" | custom-call | tf_op jit(solution)/shard_map/jit(cholesky)/cholesky | solution.py:60
  257.7 11.7 %cholesky.544 = f32[128,128]{1,0:T(8,128)S(1)} custom-call(f32[128,128]{1,0:T(8,128)S(1)} %cholesky.606), custom_call_target="Cholesky" | custom-call | tf_op jit(solution)/shard_map/jit(cholesky)/cholesky | solution.py:60
  270.1 10.0 %custom-call.68 = f32[1,128,128]{1,2,0:T(8,128)S(1)} custom-call(f32[1,128,128]{2,1,0:T(8,128)S(1)} %get-tuple-element.59), custom_call_target="InvertDiagBlocksLowerTriangular" | custom-call | tf_op jit(solution)/shard_map/jit(cholesky)/cholesky | solution.py:60
  282.7 11.7 %cholesky.562 = f32[128,128]{1,0:T(8,128)S(1)} custom-call(f32[128,128]{1,0:T(8,128)S(1)} %convolution_subtract_fusion.11), custom_call_target="Cholesky" | custom-call | tf_op jit(solution)/shard_map/jit(cholesky)/cholesky | solution.py:60
  304.8 6.6 %fusion = (f32[1024,1024]{1,0:T(8,128)}, f32[1024,1024]{1,0:T(8,128)}) fusion(f32[1024,1024]{1,0:T(8,128)} %get-tuple-element.57, pred[]{:T(512)S(6)} %cholesky.576), kind=kLoop, calls=%fused_computation.8 | loop fusion | flops 4194304 | bytes 12582913 | tf_op jit(solution)/shard_map/triangular_solve | solution.py:61
  311.4 23.2 %while.1 = (s32[]{:T(128)}, f32[1024,1024]{1,0:T(8,128)}, s32[8,2]{0,1:T(2,128)S(1)}, f32[8,128,128]{2,1,0:T(8,128)S(1)}, s32[]{:T(128)}) while((s32[]{:T(128)}, f32[1024,1024]{1,0:T(8,128)}, s32[8,2]{0,1:T(2,128)S(1)}, f32[8,128,128]{2,1,0:T(8,128)S(1)}, s32[]{:T(128)}) %tuple.65), condition=%wide.while_cond, body=%wide.while_body.sunk | while | flops 2 | bytes 131181 | solution.py:61
  334.6 79.0 %custom-call.69 = f32[8,128,128]{1,2,0:T(8,128)S(1)} custom-call(f32[8,128,128]{2,1,0:T(8,128)S(1)} %get-tuple-element.10), custom_call_target="InvertDiagBlocksLowerTriangular" | custom-call | tf_op jit(solution)/shard_map/triangular_solve | solution.py:61
  429.2 2.6 convolution_subtract_fusion.2
  433.4 2.8 convolution_subtract_fusion.1
  437.6 3.4 convolution_subtract_fusion.3
  442.5 9.0 %fusion.68 = f32[32,2048]{1,0:T(8,128)} fusion(f32[1024,2048]{1,0:T(8,128)} %all-gather.3.cloned.1.call-done, f32[1024,1024]{1,0:T(8,128)} %convolution_dynamic-update-slice_fusion, s32[]{:T(128)S(6)} %select_n.35), kind=kOutput, calls=%fused_computation.97 | convolution fusion | flops 805306368 | bytes 8781828 | tf_op jit(solution)/shard_map/dot_general | solution.py:30
  453.8 5.2 fusion.97
  459.0 99.2 %all-gather.5.cloned.1.call-done = f32[1024,2048]{1,0:T(8,128)} async-done(((f32[32,2048]{1,0:T(8,128)}), f32[1024,2048]{1,0:T(8,128)}) %all-gather.5.cloned.1.call-update) | async-done | bytes 8388624 | tf_op jit(solution)/shard_map/all_gather | solution.py:68
  558.2 7.2 %fusion.98 = f32[32,2048]{1,0:T(8,128)S(1)} fusion(f32[1024,32]{1,0:T(8,128)S(1)} %fusion.97, f32[1024,2048]{1,0:T(8,128)} %all-gather.5.cloned.1.call-done), kind=kOutput, calls=%fused_computation.199 | convolution fusion | flops 805306368 | bytes 8781824 | tf_op jit(solution)/shard_map/dot_general | solution.py:36
  (103 shorter events, 89.6 us)
Async XLA Ops:
  7.2 435.4 %all-gather.3.cloned.1.call-start = ((), (), s32[]{:S(2)}) async-start(), calls=%async_computation | async-start | bytes 8650752 | tf_op jit(solution)/shard_map/all_gather | solution.py:67
  36.2 522.0 %all-gather.5.cloned.1.call-start = ((), (), s32[]{:S(2)}) async-start(), calls=%async_computation.1 | async-start | bytes 8650752 | tf_op jit(solution)/shard_map/all_gather | solution.py:68
  83.7 2.0 copy-start
  98.8 2.0 copy-start.1
  442.5 10.7 %copy-start.3 = (f32[64]{0:T(128)S(1)}, f32[64]{0:T(128)}, u32[]{:S(2)}) copy-start(f32[64]{0:T(128)} %param.5) | copy-start | bytes 772
  459.0 106.4 %copy-start.2 = (f32[64,2048]{1,0:T(8,128)S(1)}, f32[64,2048]{1,0:T(8,128)}, u32[]{:S(2)}) copy-start(f32[64,2048]{1,0:T(8,128)} %param.3) | copy-start | bytes 1572868
Sparse Core Ops, SparseCore 0:
  36.4 101.4 all-gather.2
  451.7 106.4 all-gather.4
where the time goes:
time: 581 us; the launch traced here: 574 us
  other arithmetic  269 us (46%)
  waiting for transfers between devices  99.2 us (17%)
  matrix products  80.5 us (14%)
  blocking collectives  66.1 us (11%)
  local copies, waits for them, and re-layouts  38.5 us (7%)
  between operations  19.8 us (3%)
    another operation x30, other arithmetic, body(): diag_full = jnp.linalg.cholesky(diag_block)  172 us
    all_gather x1, waiting for transfers between devices, body(): lax.all_gather(panel_tile, 'col', axis=0, tiled=True)  99.2 us
    another operation x3, other arithmetic, body(): lax.linalg.triangular_solve(diag_full, identity, left_side=True, lower=True)  85.6 us
    all_gather x1, blocking collectives, body(): all_panel = lax.all_gather(panel_points, 'col', axis=1, tiled=True)  42.3 us
    another operation x15, matrix products, body(): lax.linalg.triangular_solve(diag_full, identity, left_side=True, lower=True)  28.1 us
    psum x1, blocking collectives, spread(): return lax.psum(block, axis)  23.8 us
    another operation x24, local copies, waits for them, and re-layouts  23 us
    another operation x14, matrix products, body(): diag_full = jnp.linalg.cholesky(diag_block)  23 us
  transfers between devices with their start and end apart: 2, of which 1 were waited for; matrix products, arithmetic and copies ran while one was open for 63% of the time, Pallas kernels for 0%

commit v1 on v0

--- a/solution.py
+++ b/solution.py
@@ -50,7 +50,9 @@
     col_share = B // n_col
     row_share = B // n_row
     rows_dev = row_points.shape[1]
-    all_panel = lax.all_gather(panel_points, "col", axis=1, tiled=True)
+    all_panel = jnp.concatenate(
+        lax.all_to_all(jnp.stack([panel_points] * lax.axis_size("col")), "col", 0, 0), axis=1
+    )
     first_col = col_index * col_share
     root_row = first_col // rows_dev
     local_look = lax.dynamic_slice_in_dim(row_points, first_col % rows_dev, col_share, 1)

time: 581 us -> 554 us (0.954)
  blocking collectives: 66.1 us -> 23.8 us
  starting transfers between devices: 0.08 us -> 11.1 us
    all_gather x1 -> x0, blocking collectives: 42.3 us -> none  [body(): all_panel = lax.all_gather(panel_points, 'col', axis=1, tiled=True)]
    all_to_all x0 -> x1, starting transfers between devices: none -> 11 us  [body(): lax.all_to_all(jnp.stack([panel_points] * lax.axis_size('col')), 'col', 0...]
    all_gather x1, waiting for transfers between devices: 99.2 us -> 90 us  [body(): lax.all_gather(panel_tile, 'col', axis=0, tiled=True)]
    all_to_all x0 -> x1, waiting for transfers between devices: none -> 7.54 us  [body(): lax.all_to_all(jnp.stack([panel_points] * lax.axis_size('col')), 'col', 0...]
  transfers between devices with their start and end apart: 2 -> 3, of which waited for: 1 -> 2; matrix products, arithmetic and copies ran while one was open for 63% -> 67% of each run, Pallas kernels for 0% -> 0%
where the time goes in v1:
time: 554 us; the launch traced here: 546 us
  other arithmetic  272 us (49%)
  waiting for transfers between devices  97.6 us (18%)
  matrix products  80.1 us (14%)
  local copies, waits for them, and re-layouts  41.1 us (7%)
  blocking collectives  23.8 us (4%)
  between operations  19.9 us (4%)
  starting transfers between devices  11.1 us (2%)
    another operation x30, other arithmetic, body(): diag_full = jnp.linalg.cholesky(diag_block)  172 us
    all_gather x1, waiting for transfers between devices, body(): lax.all_gather(panel_tile, 'col', axis=0, tiled=True)  90 us
    another operation x3, other arithmetic, body(): lax.linalg.triangular_solve(diag_full, identity, left_side=True, lower=True)  85.6 us
    another operation x15, matrix products, body(): lax.linalg.triangular_solve(diag_full, identity, left_side=True, lower=True)  28.4 us
    psum x1, blocking collectives, spread(): return lax.psum(block, axis)  23.8 us
    another operation x24, local copies, waits for them, and re-layouts  23 us
    another operation x14, matrix products, body(): diag_full = jnp.linalg.cholesky(diag_block)  22.9 us
    dot_general x2, matrix products, times_left(): jnp.dot(matrix, pieces, precision=lax.Precision.HIGHEST, preferred_elemen...  14.2 us
  transfers between devices with their start and end apart: 3, of which 2 were waited for; matrix products, arithmetic and copies ran while one was open for 67% of the time, Pallas kernels for 0%

profile of v1, /device:TPU:1, one launch (start us, length us, event | category | flops | bytes accessed | tf_op | source)
XLA Modules:
  0.0 545.6 jit_solution(8322912477117681436)
XLA Ops:
  8.1 23.8 %psum.7 = f32[64,32]{0,1:T(8,128)S(1)} all-reduce(f32[64,32]{0,1:T(8,128)S(1)} %broadcast_select_fusion), channel_id=1, replica_groups=mesh['row'=8,'col'=32] {'row'}, use_global_device_ids=true, to_apply=%region_20.21 | all-reduce | flops 2048 | bytes 16384 | tf_op jit(solution)/shard_map/psum | solution.py:12
  38.1 11.0 %all-to-all-start = ((f32[32,1,2048]{2,1,0:T(1,128)}), f32[32,1,2048]{2,1,0:T(1,128)S(1)}, u32[]{:S(2)}, u32[]{:S(2)}) async-start(f32[32,1,2048]{2,1,0:T(1,128)} %reshape.131), calls=%async_computation | async-start | bytes 524288 | tf_op jit(solution)/shard_map/all_to_all | solution.py:54
  52.0 7.5 %all-to-all-done = f32[32,1,2048]{2,1,0:T(1,128)S(1)} async-done(((f32[32,1,2048]{2,1,0:T(1,128)}), f32[32,1,2048]{2,1,0:T(1,128)S(1)}, u32[]{:S(2)}, u32[]{:S(2)}) %all-to-all-start) | async-done | bytes 262176 | tf_op jit(solution)/shard_map/all_to_all | solution.py:54
  62.0 3.4 fusion.96
  67.4 2.7 fusion.1
  70.1 5.4 copy.17
  75.5 4.9 add_multiply_fusion
  82.4 11.7 %cholesky.222 = f32[128,128]{1,0:T(8,128)S(1)} custom-call(f32[128,128]{1,0:T(8,128)S(1)} %cholesky.577), custom_call_target="Cholesky" | custom-call | tf_op jit(solution)/shard_map/jit(cholesky)/cholesky | solution.py:62
  94.2 9.8 %custom-call.62 = f32[1,128,128]{1,2,0:T(8,128)S(1)} custom-call(f32[1,128,128]{2,1,0:T(8,128)S(1)} %get-tuple-element.81), custom_call_target="InvertDiagBlocksLowerTriangular" | custom-call | tf_op jit(solution)/shard_map/jit(cholesky)/cholesky | solution.py:62
  110.3 11.7 %cholesky.243 = f32[128,128]{1,0:T(8,128)S(1)} custom-call(f32[128,128]{1,0:T(8,128)S(1)} %cholesky.581), custom_call_target="Cholesky" | custom-call | tf_op jit(solution)/shard_map/jit(cholesky)/cholesky | solution.py:62
  123.5 10.0 %custom-call.63 = f32[1,128,128]{1,2,0:T(8,128)S(1)} custom-call(f32[1,128,128]{2,1,0:T(8,128)S(1)} %get-tuple-element.78), custom_call_target="InvertDiagBlocksLowerTriangular" | custom-call | tf_op jit(solution)/shard_map/jit(cholesky)/cholesky | solution.py:62
  136.8 11.7 %cholesky.466 = f32[128,128]{1,0:T(8,128)S(1)} custom-call(f32[128,128]{1,0:T(8,128)S(1)} %cholesky.586), custom_call_target="Cholesky" | custom-call | tf_op jit(solution)/shard_map/jit(cholesky)/cholesky | solution.py:62
  149.2 9.8 %custom-call.64 = f32[1,128,128]{1,2,0:T(8,128)S(1)} custom-call(f32[1,128,128]{2,1,0:T(8,128)S(1)} %get-tuple-element.75), custom_call_target="InvertDiagBlocksLowerTriangular" | custom-call | tf_op jit(solution)/shard_map/jit(cholesky)/cholesky | solution.py:62
  162.5 12.1 %cholesky.485 = f32[128,128]{1,0:T(8,128)S(1)} custom-call(f32[128,128]{1,0:T(8,128)S(1)} %cholesky.591), custom_call_target="Cholesky" | custom-call | tf_op jit(solution)/shard_map/jit(cholesky)/cholesky | solution.py:62
  175.3 9.8 %custom-call.65 = f32[1,128,128]{1,2,0:T(8,128)S(1)} custom-call(f32[1,128,128]{2,1,0:T(8,128)S(1)} %get-tuple-element.72), custom_call_target="InvertDiagBlocksLowerTriangular" | custom-call | tf_op jit(solution)/shard_map/jit(cholesky)/cholesky | solution.py:62
  188.5 11.7 %cholesky.504 = f32[128,128]{1,0:T(8,128)S(1)} custom-call(f32[128,128]{1,0:T(8,128)S(1)} %cholesky.596), custom_call_target="Cholesky" | custom-call | tf_op jit(solution)/shard_map/jit(cholesky)/cholesky | solution.py:62
  200.9 9.8 %custom-call.66 = f32[1,128,128]{1,2,0:T(8,128)S(1)} custom-call(f32[1,128,128]{2,1,0:T(8,128)S(1)} %get-tuple-element.69), custom_call_target="InvertDiagBlocksLowerTriangular" | custom-call | tf_op jit(solution)/shard_map/jit(cholesky)/cholesky | solution.py:62
  214.2 11.7 %cholesky.524 = f32[128,128]{1,0:T(8,128)S(1)} custom-call(f32[128,128]{1,0:T(8,128)S(1)} %cholesky.601), custom_call_target="Cholesky" | custom-call | tf_op jit(solution)/shard_map/jit(cholesky)/cholesky | solution.py:62
  226.6 9.8 %custom-call.67 = f32[1,128,128]{1,2,0:T(8,128)S(1)} custom-call(f32[1,128,128]{2,1,0:T(8,128)S(1)} %get-tuple-element.66), custom_call_target="InvertDiagBlocksLowerTriangular" | custom-call | tf_op jit(solution)/shard_map/jit(cholesky)/cholesky | solution.py:62
  239.3 11.7 %cholesky.544 = f32[128,128]{1,0:T(8,128)S(1)} custom-call(f32[128,128]{1,0:T(8,128)S(1)} %cholesky.606), custom_call_target="Cholesky" | custom-call | tf_op jit(solution)/shard_map/jit(cholesky)/cholesky | solution.py:62
  251.7 10.0 %custom-call.68 = f32[1,128,128]{1,2,0:T(8,128)S(1)} custom-call(f32[1,128,128]{2,1,0:T(8,128)S(1)} %get-tuple-element.63), custom_call_target="InvertDiagBlocksLowerTriangular" | custom-call | tf_op jit(solution)/shard_map/jit(cholesky)/cholesky | solution.py:62
  264.3 11.7 %cholesky.562 = f32[128,128]{1,0:T(8,128)S(1)} custom-call(f32[128,128]{1,0:T(8,128)S(1)} %convolution_subtract_fusion.11), custom_call_target="Cholesky" | custom-call | tf_op jit(solution)/shard_map/jit(cholesky)/cholesky | solution.py:62
  286.4 6.6 %fusion = (f32[1024,1024]{1,0:T(8,128)}, f32[1024,1024]{1,0:T(8,128)}) fusion(f32[1024,1024]{1,0:T(8,128)} %get-tuple-element.61, pred[]{:T(512)S(6)} %cholesky.576), kind=kLoop, calls=%fused_computation.8 | loop fusion | flops 4194304 | bytes 12582913 | tf_op jit(solution)/shard_map/triangular_solve | solution.py:63
  293.0 23.2 %while.1 = (s32[]{:T(128)}, f32[1024,1024]{1,0:T(8,128)}, s32[8,2]{0,1:T(2,128)S(1)}, f32[8,128,128]{2,1,0:T(8,128)S(1)}, s32[]{:T(128)}) while((s32[]{:T(128)}, f32[1024,1024]{1,0:T(8,128)}, s32[8,2]{0,1:T(2,128)S(1)}, f32[8,128,128]{2,1,0:T(8,128)S(1)}, s32[]{:T(128)}) %tuple.67), condition=%wide.while_cond, body=%wide.while_body.sunk | while | flops 2 | bytes 131181 | solution.py:63
  316.2 79.0 %custom-call.69 = f32[8,128,128]{1,2,0:T(8,128)S(1)} custom-call(f32[8,128,128]{2,1,0:T(8,128)S(1)} %get-tuple-element.10), custom_call_target="InvertDiagBlocksLowerTriangular" | custom-call | tf_op jit(solution)/shard_map/triangular_solve | solution.py:63
  410.4 2.6 convolution_subtract_fusion.2
  414.5 2.8 convolution_subtract_fusion.1
  418.8 3.4 convolution_subtract_fusion.3
  423.6 9.0 %fusion.67 = f32[32,2048]{1,0:T(8,128)} fusion(f32[1024,2048]{1,0:T(8,128)} %all-gather.3.cloned.1.call-done, f32[1024,1024]{1,0:T(8,128)} %convolution_dynamic-update-slice_fusion, s32[]{:T(128)S(6)} %select_n.35), kind=kOutput, calls=%fused_computation.97 | convolution fusion | flops 805306368 | bytes 8781828 | tf_op jit(solution)/shard_map/dot_general | solution.py:30
  434.9 5.2 fusion.97
  440.1 90.0 %all-gather.5.cloned.1.call-done = f32[1024,2048]{1,0:T(8,128)} async-done(((f32[32,2048]{1,0:T(8,128)}), f32[1024,2048]{1,0:T(8,128)}) %all-gather.5.cloned.1.call-update) | async-done | bytes 8388624 | tf_op jit(solution)/shard_map/all_gather | solution.py:70
  530.2 7.2 %fusion.98 = f32[32,2048]{1,0:T(8,128)S(1)} fusion(f32[1024,32]{1,0:T(8,128)S(1)} %fusion.97, f32[1024,2048]{1,0:T(8,128)} %all-gather.5.cloned.1.call-done), kind=kOutput, calls=%fused_computation.201 | convolution fusion | flops 805306368 | bytes 8781824 | tf_op jit(solution)/shard_map/dot_general | solution.py:36
  (113 shorter events, 97.7 us)
Async XLA Ops:
  7.2 416.5 %all-gather.3.cloned.1.call-start = ((), (), s32[]{:S(2)}) async-start(), calls=%async_computation.1 | async-start | bytes 8650752 | tf_op jit(solution)/shard_map/all_gather | solution.py:69
  36.2 25.3 %copy-start.4 = (f32[64]{0:T(128)S(1)}, f32[64]{0:T(128)}, u32[]{:S(2)}) copy-start(f32[64]{0:T(128)} %param.5) | copy-start | bytes 772
  38.1 21.5 %all-to-all-start = ((f32[32,1,2048]{2,1,0:T(1,128)}), f32[32,1,2048]{2,1,0:T(1,128)S(1)}, u32[]{:S(2)}, u32[]{:S(2)}) async-start(f32[32,1,2048]{2,1,0:T(1,128)} %reshape.131), calls=%async_computation | async-start | bytes 524288 | tf_op jit(solution)/shard_map/all_to_all | solution.py:54
  49.1 481.1 %all-gather.5.cloned.1.call-start = ((), (), s32[]{:S(2)}) async-start(), calls=%async_computation.2 | async-start | bytes 8650752 | tf_op jit(solution)/shard_map/all_gather | solution.py:70
  65.5 2.0 copy-start
  80.5 2.0 copy-start.2
  395.2 4.7 copy-start.1
  440.1 97.3 %copy-start.3 = (f32[64,2048]{1,0:T(8,128)S(1)}, f32[64,2048]{1,0:T(8,128)}, u32[]{:S(2)}) copy-start(f32[64,2048]{1,0:T(8,128)} %param.3) | copy-start | bytes 1572868
Sparse Core Ops, SparseCore 0:
  36.4 101.7 all-gather.2
  432.8 97.3 all-gather.4
